TPU v7x, 512 devices: a whole 4x4x16 slice. The times are simulated.
512 devices in a mesh: elem: 32 (over x_lo, z), band: 16 (over x_hi, y, core).
Axes of the slice: x: 4 (x_hi: 2, x_lo: 2; x = x_hi * 2 + x_lo), y: 4, z: 16, core: 2. Of those that a mesh axis runs over, the one named last changes fastest.
Arguments:
- basis_sizes: int32 [512], P('elem'), may hold values from 96 to 160, as said below
- coupling_pattern: int32 [512], P('elem'), may hold values 0 or 1
- h_diag: bfloat16 [512, 160, 160], P('elem'), may hold values from -0.6708204 to 0.6708204, as said below
- h_couple: bfloat16 [512, 160, 160], P('elem'), may hold values from -0.25 to 0.25
- bands: bfloat16 [1024, 81920], P('band', 'elem'), may hold values from -1500 to 1500
Outputs:
- filtered: bfloat16 [1024, 81920], P('band', 'elem')
Inputs may be any that keep to these rules, and one draw needn't show every extreme that they name: `basis_sizes`: every element has between 96 and 160 basis functions; some element has exactly 160 and some exactly 96. `h_diag`: each block is symmetric.
All inputs are finite; a program needn't handle non-finite values. No bound on the sum of `coupling_pattern` on one device may be relied on, other than what follows from the above.
Results may differ from a plain program's by a relative error of at most 0.0085.
Values may be sent and summed in bfloat16 or wider, within the bound.
A program may use at most 64 MiB of HBM per device.

v0:
```python
import math
import jax
import jax.numpy as jnp
from jax import lax
from jax.sharding import PartitionSpec as P

DEGREE = 6
center_shift = 0.4
half_width = 2.8
epsilon_norm = 1e-06


def from_behind(value, axis, steps):
    count = lax.axis_size(axis)
    pairs = [(source, (source + steps) % count) for source in range(count)]
    return lax.ppermute(value, axis, pairs)


def with_halo(array, sides, width):
    for axis, dim in sides:
        count, length = (lax.axis_size(axis), array.shape[dim])
        up = [(i, (i + 1) % count) for i in range(count)]
        down = [(j, i) for i, j in up]
        last = lax.slice_in_dim(array, length - width, length, axis=dim)
        leading = lax.slice_in_dim(array, 0, width, axis=dim)
        before = lax.ppermute(last, axis, up)
        after = lax.ppermute(leading, axis, down)
        array = jnp.concatenate([before, array, after], axis=dim)
    return array


def cut_along(array, dim, count):
    before, after = (array.shape[:dim], array.shape[dim + 1 :])
    return jnp.moveaxis(array.reshape(*before, count, -1, *after), dim, 0)


def sent_and_summed(array, axis, dim):
    pieces = cut_along(array, dim, lax.axis_size(axis))
    arrived = lax.all_to_all(pieces, axis, split_axis=0, concat_axis=0, tiled=True)
    return arrived.sum(axis=0)


def padded_to(lines, count):
    spare = -len(lines) % count
    return jnp.pad(lines, [(0, spare)] + [(0, 0)] * (lines.ndim - 1))


def in_order(pieces, dim):
    pieces = jnp.moveaxis(pieces, 0, dim)
    dims = pieces.shape
    return pieces.reshape(*dims[:dim], dims[dim] * dims[dim + 1], *dims[dim + 2 :])


def from_everyone(array, axis):
    count = lax.axis_size(axis)
    return lax.all_to_all(
        jnp.broadcast_to(array[None], (count, *array.shape)), axis, 0, 0, tiled=True
    )


def gathered_copies(array, axis, dim):
    return in_order(from_everyone(array, axis), dim)


def nested_sum(array, axes):
    own = sent_and_summed(padded_to(array, lax.axis_size(axes)), axes, 0)
    whole = gathered_copies(own, axes, 0)
    return whole[: len(array)].reshape(array.shape)


def in_one(arrays, axis):
    line, at, done = (jnp.concatenate([a.reshape(-1) for a in arrays]), 0, [])
    running = nested_sum(line, axis)
    for a in arrays:
        done.append(running[at : at + a.size].reshape(a.shape))
        at += a.size
    return tuple(done)


def identity_block(shape, offset):
    row_ids = lax.broadcasted_iota(jnp.int32, shape, 0) + offset
    col_ids = lax.broadcasted_iota(jnp.int32, shape, 1)
    return (row_ids == col_ids).astype(jnp.float32)


def rotation_columns(gram_strip, scales, offset, total_rows):
    own_scales = lax.dynamic_slice_in_dim(scales, offset, gram_strip.shape[0], 0)
    identity = identity_block(gram_strip.shape, offset)
    normed = own_scales[:, None] * gram_strip * scales[None, :]
    return (math.sqrt(total_rows) * scales[None, :] * (1.5 * identity - 0.5 * normed)).astype(
        jnp.bfloat16
    )


def shards(basis_sizes, coupling_pattern, h_diag, h_couple, bands):
    elem_local = h_diag.shape[0]
    basis_width = h_diag.shape[1]
    band_local = bands.shape[0]
    total_rows = elem_local * lax.axis_size("elem") * basis_width
    columns = lax.broadcasted_iota(jnp.int32, (elem_local, basis_width), 1)
    valid_rows = (columns < basis_sizes[:, None]).astype(jnp.float32)
    coupling = h_couple * coupling_pattern.astype(jnp.bfloat16)[:, None, None]
    current = (
        bands.reshape(band_local, elem_local, basis_width) * valid_rows.astype(jnp.bfloat16)[None]
    )
    prior_block = from_behind(coupling[-1], "elem", 1)
    behind = jnp.concatenate([prior_block[None], coupling[:-1]], axis=0)
    previous = current
    for degree in range(DEGREE):
        current_float = current.astype(jnp.float32)
        local_term = jnp.einsum("eij,bej->bei", h_diag, current, preferred_element_type=jnp.float32)
        rimmed = with_halo(current, (("elem", 1),), 1)
        upper_term = jnp.einsum(
            "eij,bej->bei", coupling, rimmed[:, 2:], preferred_element_type=jnp.float32
        )
        lower_term = jnp.einsum(
            "eji,bej->bei", behind, rimmed[:, :-2], preferred_element_type=jnp.float32
        )
        applied = (local_term + upper_term + lower_term) * valid_rows[None]
        shifted = applied - center_shift * current_float
        if degree == 0:
            next_iterate = shifted / half_width
        else:
            next_iterate = 2.0 * shifted / half_width - previous.astype(jnp.float32)
        previous, current = (current, next_iterate.astype(jnp.bfloat16))
    filtered = current.reshape(band_local, elem_local * basis_width)
    every_band = lax.all_gather(filtered, "band", axis=0, tiled=True)
    strip = lax.dot_general(
        filtered, every_band, (((1,), (1,)), ((), ())), preferred_element_type=jnp.float32
    )
    squares = jnp.sum(jnp.square(every_band.astype(jnp.float32)), axis=1)
    strip, squares = in_one((strip, squares), "elem")
    scales = lax.rsqrt(squares + epsilon_norm)
    offset = lax.axis_index("band") * band_local
    weights = rotation_columns(strip, scales, offset, total_rows)
    return jnp.dot(weights, every_band, preferred_element_type=jnp.float32).astype(jnp.bfloat16)


def solution(mesh):
    in_specs = (
        P("elem"),
        P("elem"),
        P("elem", None, None),
        P("elem", None, None),
        P("band", "elem"),
    )
    out_specs = P("band", "elem")
    return jax.shard_map(shards, mesh=mesh, in_specs=in_specs, out_specs=out_specs, check_vma=False)
```

profile of v0, /device:TPU:4, one launch (start us, length us, event | category | flops | bytes accessed | tf_op | source)
XLA Modules:
  0.0 235.6 jit_solution(5489966992753871043)
XLA Ops:
  6.5 0.9 fusion.79
  7.4 1.6 reshape.59
  9.0 0.2 copy_multiply_fusion
  9.2 3.8 %collective-permute-start.1 = (bf16[64,1,160]{2,0,1:T(8,128)(2,1)S(1)}, bf16[64,1,160]{2,0,1:T(8,128)(2,1)S(1)}, u32[]{:S(2)}, u32[]{:S(2)}) collective-permute-start(bf16[64,1,160]{2,0,1:T(8,128)(2,1)S(1)} %get-tuple-element.15), channel_id=1, source_target_pairs={{0,16},{16,32},{32,48},{48,64},{64,80},{80,96},{96,112},{112,128},... | collective-permute-start | bytes 61448 | tf_op jit(solution)/shard_map/ppermute | solution.py:26
  13.0 10.1 %collective-permute-start = (bf16[64,1,160]{2,0,1:T(8,128)(2,1)S(1)}, bf16[64,1,160]{2,0,1:T(8,128)(2,1)S(1)}, u32[]{:S(2)}, u32[]{:S(2)}) collective-permute-start(bf16[64,1,160]{2,0,1:T(8,128)(2,1)S(1)} %get-tuple-element.16), channel_id=1, source_target_pairs={{16,0},{32,16},{48,32},{64,48},{80,64},{96,80},{112,96},{128,112},... | collective-permute-start | bytes 61448 | tf_op jit(solution)/shard_map/ppermute | solution.py:27
  23.2 0.2 broadcast_multiply_fusion
  23.4 1.9 collective-permute-start.2
  25.3 0.6 fusion.103
  25.9 0.1 slice.131
  26.0 0.0 collective-permute-done
  26.0 0.5 convolution_add_fusion.11
  26.5 0.0 collective-permute-done.1
  26.5 5.3 %collective-permute-done.2 = bf16[160,160]{1,0:T(8,128)(2,1)S(1)} collective-permute-done((bf16[160,160]{1,0:T(8,128)(2,1)S(1)}, bf16[160,160]{1,0:T(8,128)(2,1)S(1)}, u32[]{:S(2)}, u32[]{:S(2)}) %collective-permute-start.2) | collective-permute-done | bytes 51232 | tf_op jit(solution)/shard_map/ppermute | solution.py:16
  31.8 0.4 fusion.24
  32.3 1.9 collective-permute-start.3
  34.2 0.6 fusion.104
  34.8 3.9 %collective-permute-start.4 = (bf16[64,1,160]{2,0,1:T(8,128)(2,1)S(1)}, bf16[64,1,160]{2,0,1:T(8,128)(2,1)S(1)}, u32[]{:S(2)}, u32[]{:S(2)}) collective-permute-start(bf16[64,1,160]{2,0,1:T(8,128)(2,1)S(1)} %get-tuple-element.13), channel_id=1, source_target_pairs={{0,16},{16,32},{32,48},{48,64},{64,80},{80,96},{96,112},{112,128},... | collective-permute-start | bytes 61448 | tf_op jit(solution)/shard_map/ppermute | solution.py:26
  38.7 0.0 collective-permute-done.3
  38.7 0.5 convolution_add_fusion.9
  39.3 3.4 %collective-permute-done.4 = bf16[64,1,160]{2,0,1:T(8,128)(2,1)S(1)} collective-permute-done((bf16[64,1,160]{2,0,1:T(8,128)(2,1)S(1)}, bf16[64,1,160]{2,0,1:T(8,128)(2,1)S(1)}, u32[]{:S(2)}, u32[]{:S(2)}) %collective-permute-start.4) | collective-permute-done | bytes 20512 | tf_op jit(solution)/shard_map/ppermute | solution.py:26
  42.7 0.5 fusion.25
  43.2 1.9 collective-permute-start.5
  45.2 0.6 fusion.105
  45.7 3.9 %collective-permute-start.6 = (bf16[64,1,160]{2,0,1:T(8,128)(2,1)S(1)}, bf16[64,1,160]{2,0,1:T(8,128)(2,1)S(1)}, u32[]{:S(2)}, u32[]{:S(2)}) collective-permute-start(bf16[64,1,160]{2,0,1:T(8,128)(2,1)S(1)} %get-tuple-element.11), channel_id=1, source_target_pairs={{0,16},{16,32},{32,48},{48,64},{64,80},{80,96},{96,112},{112,128},... | collective-permute-start | bytes 61448 | tf_op jit(solution)/shard_map/ppermute | solution.py:26
  49.6 0.0 collective-permute-done.5
  49.7 0.5 convolution_add_fusion.7
  50.2 3.4 %collective-permute-done.6 = bf16[64,1,160]{2,0,1:T(8,128)(2,1)S(1)} collective-permute-done((bf16[64,1,160]{2,0,1:T(8,128)(2,1)S(1)}, bf16[64,1,160]{2,0,1:T(8,128)(2,1)S(1)}, u32[]{:S(2)}, u32[]{:S(2)}) %collective-permute-start.6) | collective-permute-done | bytes 20512 | tf_op jit(solution)/shard_map/ppermute | solution.py:26
  53.6 0.5 fusion.26
  54.2 1.9 collective-permute-start.7
  56.1 0.6 fusion.106
  56.6 3.9 %collective-permute-start.8 = (bf16[64,1,160]{2,0,1:T(8,128)(2,1)S(1)}, bf16[64,1,160]{2,0,1:T(8,128)(2,1)S(1)}, u32[]{:S(2)}, u32[]{:S(2)}) collective-permute-start(bf16[64,1,160]{2,0,1:T(8,128)(2,1)S(1)} %get-tuple-element.9), channel_id=1, source_target_pairs={{0,16},{16,32},{32,48},{48,64},{64,80},{80,96},{96,112},{112,128},... | collective-permute-start | bytes 61448 | tf_op jit(solution)/shard_map/ppermute | solution.py:26
  60.6 0.5 convolution_add_fusion.5
  61.1 3.4 %collective-permute-done.8 = bf16[64,1,160]{2,0,1:T(8,128)(2,1)S(1)} collective-permute-done((bf16[64,1,160]{2,0,1:T(8,128)(2,1)S(1)}, bf16[64,1,160]{2,0,1:T(8,128)(2,1)S(1)}, u32[]{:S(2)}, u32[]{:S(2)}) %collective-permute-start.8) | collective-permute-done | bytes 20512 | tf_op jit(solution)/shard_map/ppermute | solution.py:26
  64.6 0.5 fusion.27
  65.1 1.9 collective-permute-start.9
  67.0 0.6 fusion.107
  67.6 3.9 %collective-permute-start.10 = (bf16[64,1,160]{2,0,1:T(8,128)(2,1)S(1)}, bf16[64,1,160]{2,0,1:T(8,128)(2,1)S(1)}, u32[]{:S(2)}, u32[]{:S(2)}) collective-permute-start(bf16[64,1,160]{2,0,1:T(8,128)(2,1)S(1)} %get-tuple-element.7), channel_id=1, source_target_pairs={{0,16},{16,32},{32,48},{48,64},{64,80},{80,96},{96,112},{112,128},... | collective-permute-start | bytes 61448 | tf_op jit(solution)/shard_map/ppermute | solution.py:26
  71.5 0.0 collective-permute-done.9
  71.5 0.5 convolution_add_fusion.3
  72.0 3.4 %collective-permute-done.10 = bf16[64,1,160]{2,0,1:T(8,128)(2,1)S(1)} collective-permute-done((bf16[64,1,160]{2,0,1:T(8,128)(2,1)S(1)}, bf16[64,1,160]{2,0,1:T(8,128)(2,1)S(1)}, u32[]{:S(2)}, u32[]{:S(2)}) %collective-permute-start.10) | collective-permute-done | bytes 20512 | tf_op jit(solution)/shard_map/ppermute | solution.py:26
  75.5 0.5 fusion.28
  76.0 1.9 collective-permute-start.11
  77.9 0.6 fusion.108
  78.5 4.1 %collective-permute-start.12 = (bf16[64,1,160]{2,0,1:T(8,128)(2,1)S(1)}, bf16[64,1,160]{2,0,1:T(8,128)(2,1)S(1)}, u32[]{:S(2)}, u32[]{:S(2)}) collective-permute-start(bf16[64,1,160]{2,0,1:T(8,128)(2,1)S(1)} %get-tuple-element.5), channel_id=1, source_target_pairs={{0,16},{16,32},{32,48},{48,64},{64,80},{80,96},{96,112},{112,128},... | collective-permute-start | bytes 61448 | tf_op jit(solution)/shard_map/ppermute | solution.py:26
  82.6 0.5 convolution_add_fusion.1
  83.1 3.3 %collective-permute-done.12 = bf16[64,1,160]{2,0,1:T(8,128)(2,1)S(1)} collective-permute-done((bf16[64,1,160]{2,0,1:T(8,128)(2,1)S(1)}, bf16[64,1,160]{2,0,1:T(8,128)(2,1)S(1)}, u32[]{:S(2)}, u32[]{:S(2)}) %collective-permute-start.12) | collective-permute-done | bytes 20512 | tf_op jit(solution)/shard_map/ppermute | solution.py:26
  86.4 0.5 fusion.29
  86.9 0.3 copy.11
  87.2 1.5 reshape.60
  88.7 0.0 all-gather.2.cloned.1.call-update
  88.7 64.4 %all-gather.2.cloned.1.call-done = bf16[1024,2560]{1,0:T(8,128)(2,1)} async-done(((bf16[64,2560]{1,0:T(8,128)(2,1)}), bf16[1024,2560]{1,0:T(8,128)(2,1)}) %all-gather.2.cloned.1.call-update) | async-done | bytes 5242896 | tf_op jit(solution)/shard_map/all_gather | solution.py:127
  153.1 4.4 %convolution_bitcast_fusion = f32[8,8,8,128]{3,2,1,0:T(8,128)S(1)} fusion(bf16[64,2560]{1,0:T(8,128)(2,1)} %reshape.60, bf16[1024,2560]{1,0:T(8,128)(2,1)} %all-gather.2.cloned.1.call-done), kind=kOutput, calls=%fused_computation.55 | convolution fusion | flops 335544320 | bytes 5832704 | tf_op jit(solution)/shard_map/dot_general | solution.py:128
  157.6 1.1 multiply_reduce_fusion
  158.7 0.4 all_to_all.10
  159.1 37.1 %all_to_all.15 = f32[32,1,2080]{2,1,0:T(1,128)S(1)} all-to-all(f32[32,1,2080]{2,1,0:T(1,128)S(1)} %all_to_all.10), channel_id=1, replica_groups=mesh['elem'=32,'band'=16] {'elem'}, dimensions={0} | all-to-all | bytes 532480 | tf_op jit(solution)/shard_map/all_to_all | solution.py:39
  196.1 0.2 reduce_sum.19
  196.3 0.9 broadcast_in_dim.5
  197.1 3.9 %all-to-all-start.1 = ((f32[32,1,2080]{2,1,0:T(1,128)}), f32[32,1,2080]{2,1,0:T(1,128)S(1)}, u32[]{:S(2)}, u32[]{:S(2)}) async-start(f32[32,1,2080]{2,1,0:T(1,128)} %broadcast_in_dim.5), calls=%async_computation.1 | async-start | bytes 557056 | tf_op jit(solution)/shard_map/all_to_all | solution.py:56
  201.0 22.1 %all-to-all-done.1 = f32[32,1,2080]{2,1,0:T(1,128)S(1)} async-done(((f32[32,1,2080]{2,1,0:T(1,128)}), f32[32,1,2080]{2,1,0:T(1,128)S(1)}, u32[]{:S(2)}, u32[]{:S(2)}) %all-to-all-start.1) | async-done | bytes 266272 | tf_op jit(solution)/shard_map/all_to_all | solution.py:56
  223.2 0.7 reduce.1
  223.8 0.2 reshape.62
  224.1 0.3 slice.126
  224.3 0.1 dynamic_slice.3
  224.4 4.3 %convolution_convert_fusion = bf16[64,2560]{1,0:T(8,128)(2,1)} fusion(bf16[1024,2560]{1,0:T(8,128)(2,1)} %all-gather.2.cloned.1.call-done, f32[65,1024]{1,0:T(8,128)S(1)} %slice.126, f32[1024]{0:T(1024)S(1)} %get-tuple-element.18, f32[64]{0:T(128)S(1)} %dynamic_slice.3, s32[64]{0:T(128)S(1)} %iota_add_fusion, f32[1024]{0:T(1024)S(1)} %get-tuple-element.17), kind=kOutput, calls=%fused_computation.1 | convolution fusion | flops 336232448 | bytes 5841920 | tf_op jit(solution)/shard_map/dot_general | solution.py:136
  (23 shorter events, 0.2 us)
Async XLA Ops:
  6.5 18.8 %copy-start = (bf16[16,160,160]{2,1,0:T(8,128)(2,1)S(1)}, bf16[16,160,160]{2,1,0:T(8,128)(2,1)}, u32[]{:S(2)}) copy-start(bf16[16,160,160]{2,1,0:T(8,128)(2,1)} %param.7) | copy-start | bytes 2457604
  6.5 16.7 %copy-start.3 = (s32[16]{0:T(128)S(1)}, s32[16]{0:T(128)}, u32[]{:S(2)}) copy-start(s32[16]{0:T(128)} %param.6) | copy-start | bytes 196
  6.5 16.7 %copy-start.2 = (bf16[16,160,160]{2,1,0:T(8,128)(2,1)S(1)}, bf16[16,160,160]{2,1,0:T(8,128)(2,1)}, u32[]{:S(2)}) copy-start(bf16[16,160,160]{2,1,0:T(8,128)(2,1)} %param.8) | copy-start | bytes 2457604
  6.5 146.5 %all-gather.2.cloned.1.call-start = ((), (), s32[]{:S(2)}) async-start(), calls=%async_computation.2 | async-start | bytes 5570560 | tf_op jit(solution)/shard_map/all_gather | solution.py:127
  9.2 17.3 %collective-permute-start.1 = (bf16[64,1,160]{2,0,1:T(8,128)(2,1)S(1)}, bf16[64,1,160]{2,0,1:T(8,128)(2,1)S(1)}, u32[]{:S(2)}, u32[]{:S(2)}) collective-permute-start(bf16[64,1,160]{2,0,1:T(8,128)(2,1)S(1)} %get-tuple-element.15), channel_id=1, source_target_pairs={{0,16},{16,32},{32,48},{48,64},{64,80},{80,96},{96,112},{112,128},... | collective-permute-start | bytes 61448 | tf_op jit(solution)/shard_map/ppermute | solution.py:26
  13.0 12.9 %collective-permute-start = (bf16[64,1,160]{2,0,1:T(8,128)(2,1)S(1)}, bf16[64,1,160]{2,0,1:T(8,128)(2,1)S(1)}, u32[]{:S(2)}, u32[]{:S(2)}) collective-permute-start(bf16[64,1,160]{2,0,1:T(8,128)(2,1)S(1)} %get-tuple-element.16), channel_id=1, source_target_pairs={{16,0},{32,16},{48,32},{64,48},{80,64},{96,80},{112,96},{128,112},... | collective-permute-start | bytes 61448 | tf_op jit(solution)/shard_map/ppermute | solution.py:27
  23.4 8.4 %collective-permute-start.2 = (bf16[160,160]{1,0:T(8,128)(2,1)S(1)}, bf16[160,160]{1,0:T(8,128)(2,1)S(1)}, u32[]{:S(2)}, u32[]{:S(2)}) collective-permute-start(bf16[160,160]{1,0:T(8,128)(2,1)S(1)} %slice_bitcast_fusion), channel_id=1, source_target_pairs={{0,16},{16,32},{32,48},{48,64},{64,80},{80,96},{96,112},{112,128},... | collective-permute-start | bytes 153608 | tf_op jit(solution)/shard_map/ppermute | solution.py:16
  32.3 6.4 %collective-permute-start.3 = (bf16[64,1,160]{2,0,1:T(8,128)(2,1)S(1)}, bf16[64,1,160]{2,0,1:T(8,128)(2,1)S(1)}, u32[]{:S(2)}, u32[]{:S(2)}) collective-permute-start(bf16[64,1,160]{2,0,1:T(8,128)(2,1)S(1)} %get-tuple-element.14), channel_id=1, source_target_pairs={{16,0},{32,16},{48,32},{64,48},{80,64},{96,80},{112,96},{128,112},... | collective-permute-start | bytes 61448 | tf_op jit(solution)/shard_map/ppermute | solution.py:27
  34.8 7.9 %collective-permute-start.4 = (bf16[64,1,160]{2,0,1:T(8,128)(2,1)S(1)}, bf16[64,1,160]{2,0,1:T(8,128)(2,1)S(1)}, u32[]{:S(2)}, u32[]{:S(2)}) collective-permute-start(bf16[64,1,160]{2,0,1:T(8,128)(2,1)S(1)} %get-tuple-element.13), channel_id=1, source_target_pairs={{0,16},{16,32},{32,48},{48,64},{64,80},{80,96},{96,112},{112,128},... | collective-permute-start | bytes 61448 | tf_op jit(solution)/shard_map/ppermute | solution.py:26
  43.2 6.4 %collective-permute-start.5 = (bf16[64,1,160]{2,0,1:T(8,128)(2,1)S(1)}, bf16[64,1,160]{2,0,1:T(8,128)(2,1)S(1)}, u32[]{:S(2)}, u32[]{:S(2)}) collective-permute-start(bf16[64,1,160]{2,0,1:T(8,128)(2,1)S(1)} %get-tuple-element.12), channel_id=1, source_target_pairs={{16,0},{32,16},{48,32},{64,48},{80,64},{96,80},{112,96},{128,112},... | collective-permute-start | bytes 61448 | tf_op jit(solution)/shard_map/ppermute | solution.py:27
  45.7 7.9 %collective-permute-start.6 = (bf16[64,1,160]{2,0,1:T(8,128)(2,1)S(1)}, bf16[64,1,160]{2,0,1:T(8,128)(2,1)S(1)}, u32[]{:S(2)}, u32[]{:S(2)}) collective-permute-start(bf16[64,1,160]{2,0,1:T(8,128)(2,1)S(1)} %get-tuple-element.11), channel_id=1, source_target_pairs={{0,16},{16,32},{32,48},{48,64},{64,80},{80,96},{96,112},{112,128},... | collective-permute-start | bytes 61448 | tf_op jit(solution)/shard_map/ppermute | solution.py:26
  54.2 6.4 %collective-permute-start.7 = (bf16[64,1,160]{2,0,1:T(8,128)(2,1)S(1)}, bf16[64,1,160]{2,0,1:T(8,128)(2,1)S(1)}, u32[]{:S(2)}, u32[]{:S(2)}) collective-permute-start(bf16[64,1,160]{2,0,1:T(8,128)(2,1)S(1)} %get-tuple-element.10), channel_id=1, source_target_pairs={{16,0},{32,16},{48,32},{64,48},{80,64},{96,80},{112,96},{128,112},... | collective-permute-start | bytes 61448 | tf_op jit(solution)/shard_map/ppermute | solution.py:27
  56.6 7.9 %collective-permute-start.8 = (bf16[64,1,160]{2,0,1:T(8,128)(2,1)S(1)}, bf16[64,1,160]{2,0,1:T(8,128)(2,1)S(1)}, u32[]{:S(2)}, u32[]{:S(2)}) collective-permute-start(bf16[64,1,160]{2,0,1:T(8,128)(2,1)S(1)} %get-tuple-element.9), channel_id=1, source_target_pairs={{0,16},{16,32},{32,48},{48,64},{64,80},{80,96},{96,112},{112,128},... | collective-permute-start | bytes 61448 | tf_op jit(solution)/shard_map/ppermute | solution.py:26
  65.1 6.4 %collective-permute-start.9 = (bf16[64,1,160]{2,0,1:T(8,128)(2,1)S(1)}, bf16[64,1,160]{2,0,1:T(8,128)(2,1)S(1)}, u32[]{:S(2)}, u32[]{:S(2)}) collective-permute-start(bf16[64,1,160]{2,0,1:T(8,128)(2,1)S(1)} %get-tuple-element.8), channel_id=1, source_target_pairs={{16,0},{32,16},{48,32},{64,48},{80,64},{96,80},{112,96},{128,112},... | collective-permute-start | bytes 61448 | tf_op jit(solution)/shard_map/ppermute | solution.py:27
  67.6 7.9 %collective-permute-start.10 = (bf16[64,1,160]{2,0,1:T(8,128)(2,1)S(1)}, bf16[64,1,160]{2,0,1:T(8,128)(2,1)S(1)}, u32[]{:S(2)}, u32[]{:S(2)}) collective-permute-start(bf16[64,1,160]{2,0,1:T(8,128)(2,1)S(1)} %get-tuple-element.7), channel_id=1, source_target_pairs={{0,16},{16,32},{32,48},{48,64},{64,80},{80,96},{96,112},{112,128},... | collective-permute-start | bytes 61448 | tf_op jit(solution)/shard_map/ppermute | solution.py:26
  76.0 6.6 %collective-permute-start.11 = (bf16[64,1,160]{2,0,1:T(8,128)(2,1)S(1)}, bf16[64,1,160]{2,0,1:T(8,128)(2,1)S(1)}, u32[]{:S(2)}, u32[]{:S(2)}) collective-permute-start(bf16[64,1,160]{2,0,1:T(8,128)(2,1)S(1)} %get-tuple-element.6), channel_id=1, source_target_pairs={{16,0},{32,16},{48,32},{64,48},{80,64},{96,80},{112,96},{128,112},... | collective-permute-start | bytes 61448 | tf_op jit(solution)/shard_map/ppermute | solution.py:27
  78.5 7.9 %collective-permute-start.12 = (bf16[64,1,160]{2,0,1:T(8,128)(2,1)S(1)}, bf16[64,1,160]{2,0,1:T(8,128)(2,1)S(1)}, u32[]{:S(2)}, u32[]{:S(2)}) collective-permute-start(bf16[64,1,160]{2,0,1:T(8,128)(2,1)S(1)} %get-tuple-element.5), channel_id=1, source_target_pairs={{0,16},{16,32},{32,48},{48,64},{64,80},{80,96},{96,112},{112,128},... | collective-permute-start | bytes 61448 | tf_op jit(solution)/shard_map/ppermute | solution.py:26
  153.1 4.5 %copy-start.1 = (bf16[1024,2560]{1,0:T(8,128)(2,1)S(1)}, bf16[1024,2560]{1,0:T(8,128)(2,1)}, u32[]{:S(2)}) copy-start(bf16[1024,2560]{1,0:T(8,128)(2,1)} %all-gather.2.cloned.1.call-done) | copy-start | bytes 15728644
  197.1 26.0 %all-to-all-start.1 = ((f32[32,1,2080]{2,1,0:T(1,128)}), f32[32,1,2080]{2,1,0:T(1,128)S(1)}, u32[]{:S(2)}, u32[]{:S(2)}) async-start(f32[32,1,2080]{2,1,0:T(1,128)} %broadcast_in_dim.5), calls=%async_computation.1 | async-start | bytes 557056 | tf_op jit(solution)/shard_map/all_to_all | solution.py:56
Sparse Core Ops, SparseCore 0:
  88.8 64.1 all-gather.1
where the time goes:
time: 236 us
  waiting for transfers between devices  109 us (46%)
  starting transfers between devices  49.1 us (21%)
  blocking collectives  37.1 us (16%)
  matrix products  18.3 us (8%)
  between operations  13.8 us (6%)
  local copies, waits for them, and re-layouts  5.35 us (2%)
  other arithmetic  3.15 us (1%)
    all_gather x1, waiting for transfers between devices, shards(): every_band = lax.all_gather(filtered, 'band', axis=0, tiled=True)  64.4 us
    all_to_all x1, blocking collectives, sent_and_summed(): lax.all_to_all(pieces, axis, split_axis=0, concat_axis=0, tiled=True)  37.1 us
    ppermute x6, starting transfers between devices, with_halo(): before = lax.ppermute(last, axis, up)  23.6 us
    all_to_all x1, waiting for transfers between devices, from_everyone(): lax.all_to_all(jnp.broadcast_to(array[None], (count, *array.shape)), axis...  22.1 us
    ppermute x6, starting transfers between devices, with_halo(): after = lax.ppermute(leading, axis, down)  19.7 us
    ppermute x6, waiting for transfers between devices, with_halo(): before = lax.ppermute(last, axis, up)  17 us
    ppermute x1, waiting for transfers between devices, from_behind(): return lax.ppermute(value, axis, pairs)  5.3 us
  transfers between devices with their start and end apart: 15, of which 8 were waited for; matrix products, arithmetic and copies ran while one was open for 3% of the time, Pallas kernels for 0%

commit v1 on v0

--- a/solution.py
+++ b/solution.py
@@ -124,7 +124,10 @@
             next_iterate = 2.0 * shifted / half_width - previous.astype(jnp.float32)
         previous, current = (current, next_iterate.astype(jnp.bfloat16))
     filtered = current.reshape(band_local, elem_local * basis_width)
-    every_band = lax.all_gather(filtered, "band", axis=0, tiled=True)
+    peers = lax.axis_size("band")
+    shards_2 = jnp.stack([filtered for _ in range(peers)])
+    shards_2 = lax.all_to_all(shards_2, "band", split_axis=0, concat_axis=0)
+    every_band = jnp.concatenate(shards_2, axis=0)
     strip = lax.dot_general(
         filtered, every_band, (((1,), (1,)), ((), ())), preferred_element_type=jnp.float32
     )

time: 236 us -> 215 us (0.911)
  the two profiles are of different devices: /device:TPU:4 before, /device:TPU:24 now
where the time goes in v1:
time: 215 us; the launch traced here: 214 us
  blocking collectives  94.1 us (44%)
  starting transfers between devices  49.2 us (23%)
  waiting for transfers between devices  46.1 us (21%)
  matrix products  15.5 us (7%)
  local copies, waits for them, and re-layouts  5.74 us (3%)
  other arithmetic  3.15 us (1%)
    all_to_all x1, blocking collectives, shards(): shards_2 = lax.all_to_all(shards_2, 'band', split_axis=0, concat_axis=0)  67.4 us
    all_to_all x1, blocking collectives, sent_and_summed(): lax.all_to_all(pieces, axis, split_axis=0, concat_axis=0, tiled=True)  26.7 us
    ppermute x6, starting transfers between devices, with_halo(): after = lax.ppermute(leading, axis, down)  23.9 us
    ppermute x6, waiting for transfers between devices, with_halo(): before = lax.ppermute(last, axis, up)  23.9 us
    all_to_all x1, waiting for transfers between devices, from_everyone(): lax.all_to_all(jnp.broadcast_to(array[None], (count, *array.shape)), axis...  22.2 us
    ppermute x6, starting transfers between devices, with_halo(): before = lax.ppermute(last, axis, up)  19.5 us
    dot_general x1, matrix products, shards(): jnp.dot(weights, every_band, preferred_element_type=jnp.float32)  4.31 us
  transfers between devices with their start and end apart: 14, of which 7 were waited for; matrix products, arithmetic and copies ran while one was open for 3% of the time, Pallas kernels for 0%

profile of v1, /device:TPU:24, one launch (start us, length us, event | category | flops | bytes accessed | tf_op | source)
XLA Modules:
  0.0 214.3 jit_solution(16017049923737742627)
XLA Ops:
  0.0 0.9 fusion.79
  0.9 1.6 reshape.65
  2.5 0.2 copy_multiply_fusion
  2.7 12.3 %collective-permute-start = (bf16[64,1,160]{2,0,1:T(8,128)(2,1)S(1)}, bf16[64,1,160]{2,0,1:T(8,128)(2,1)S(1)}, u32[]{:S(2)}, u32[]{:S(2)}) collective-permute-start(bf16[64,1,160]{2,0,1:T(8,128)(2,1)S(1)} %get-tuple-element.16), channel_id=1, source_target_pairs={{16,0},{32,16},{48,32},{64,48},{80,64},{96,80},{112,96},{128,112},... | collective-permute-start | bytes 61448 | tf_op jit(solution)/shard_map/ppermute | solution.py:27
  15.0 0.2 broadcast_multiply_fusion
  15.2 1.9 collective-permute-start.2
  17.2 1.9 collective-permute-start.1
  19.1 0.6 fusion.103
  19.6 0.1 slice.131
  19.7 0.5 convolution_add_fusion.11
  20.3 4.8 %collective-permute-done.1 = bf16[64,1,160]{2,0,1:T(8,128)(2,1)S(1)} collective-permute-done((bf16[64,1,160]{2,0,1:T(8,128)(2,1)S(1)}, bf16[64,1,160]{2,0,1:T(8,128)(2,1)S(1)}, u32[]{:S(2)}, u32[]{:S(2)}) %collective-permute-start.1) | collective-permute-done | bytes 20512 | tf_op jit(solution)/shard_map/ppermute | solution.py:26
  25.1 0.0 collective-permute-done.2
  25.1 0.4 fusion.24
  25.5 3.9 %collective-permute-start.3 = (bf16[64,1,160]{2,0,1:T(8,128)(2,1)S(1)}, bf16[64,1,160]{2,0,1:T(8,128)(2,1)S(1)}, u32[]{:S(2)}, u32[]{:S(2)}) collective-permute-start(bf16[64,1,160]{2,0,1:T(8,128)(2,1)S(1)} %get-tuple-element.14), channel_id=1, source_target_pairs={{16,0},{32,16},{48,32},{64,48},{80,64},{96,80},{112,96},{128,112},... | collective-permute-start | bytes 61448 | tf_op jit(solution)/shard_map/ppermute | solution.py:27
  29.5 0.6 fusion.104
  30.0 1.9 collective-permute-start.4
  31.9 0.0 collective-permute-done.3
  32.0 0.5 convolution_add_fusion.9
  32.5 5.4 %collective-permute-done.4 = bf16[64,1,160]{2,0,1:T(8,128)(2,1)S(1)} collective-permute-done((bf16[64,1,160]{2,0,1:T(8,128)(2,1)S(1)}, bf16[64,1,160]{2,0,1:T(8,128)(2,1)S(1)}, u32[]{:S(2)}, u32[]{:S(2)}) %collective-permute-start.4) | collective-permute-done | bytes 20512 | tf_op jit(solution)/shard_map/ppermute | solution.py:26
  37.9 0.5 fusion.25
  38.5 1.9 collective-permute-start.5
  40.4 0.6 fusion.105
  40.9 3.9 %collective-permute-start.6 = (bf16[64,1,160]{2,0,1:T(8,128)(2,1)S(1)}, bf16[64,1,160]{2,0,1:T(8,128)(2,1)S(1)}, u32[]{:S(2)}, u32[]{:S(2)}) collective-permute-start(bf16[64,1,160]{2,0,1:T(8,128)(2,1)S(1)} %get-tuple-element.11), channel_id=1, source_target_pairs={{0,16},{16,32},{32,48},{48,64},{64,80},{80,96},{96,112},{112,128},... | collective-permute-start | bytes 61448 | tf_op jit(solution)/shard_map/ppermute | solution.py:26
  44.9 0.5 convolution_add_fusion.7
  45.4 3.4 %collective-permute-done.6 = bf16[64,1,160]{2,0,1:T(8,128)(2,1)S(1)} collective-permute-done((bf16[64,1,160]{2,0,1:T(8,128)(2,1)S(1)}, bf16[64,1,160]{2,0,1:T(8,128)(2,1)S(1)}, u32[]{:S(2)}, u32[]{:S(2)}) %collective-permute-start.6) | collective-permute-done | bytes 20512 | tf_op jit(solution)/shard_map/ppermute | solution.py:26
  48.9 0.5 fusion.26
  49.4 1.9 collective-permute-start.7
  51.3 0.6 fusion.106
  51.9 3.9 %collective-permute-start.8 = (bf16[64,1,160]{2,0,1:T(8,128)(2,1)S(1)}, bf16[64,1,160]{2,0,1:T(8,128)(2,1)S(1)}, u32[]{:S(2)}, u32[]{:S(2)}) collective-permute-start(bf16[64,1,160]{2,0,1:T(8,128)(2,1)S(1)} %get-tuple-element.9), channel_id=1, source_target_pairs={{0,16},{16,32},{32,48},{48,64},{64,80},{80,96},{96,112},{112,128},... | collective-permute-start | bytes 61448 | tf_op jit(solution)/shard_map/ppermute | solution.py:26
  55.8 0.5 convolution_add_fusion.5
  56.3 3.4 %collective-permute-done.8 = bf16[64,1,160]{2,0,1:T(8,128)(2,1)S(1)} collective-permute-done((bf16[64,1,160]{2,0,1:T(8,128)(2,1)S(1)}, bf16[64,1,160]{2,0,1:T(8,128)(2,1)S(1)}, u32[]{:S(2)}, u32[]{:S(2)}) %collective-permute-start.8) | collective-permute-done | bytes 20512 | tf_op jit(solution)/shard_map/ppermute | solution.py:26
  59.8 0.5 fusion.27
  60.3 1.9 collective-permute-start.9
  62.2 0.6 fusion.107
  62.8 3.9 %collective-permute-start.10 = (bf16[64,1,160]{2,0,1:T(8,128)(2,1)S(1)}, bf16[64,1,160]{2,0,1:T(8,128)(2,1)S(1)}, u32[]{:S(2)}, u32[]{:S(2)}) collective-permute-start(bf16[64,1,160]{2,0,1:T(8,128)(2,1)S(1)} %get-tuple-element.7), channel_id=1, source_target_pairs={{0,16},{16,32},{32,48},{48,64},{64,80},{80,96},{96,112},{112,128},... | collective-permute-start | bytes 61448 | tf_op jit(solution)/shard_map/ppermute | solution.py:26
  66.7 0.5 convolution_add_fusion.3
  67.3 3.4 %collective-permute-done.10 = bf16[64,1,160]{2,0,1:T(8,128)(2,1)S(1)} collective-permute-done((bf16[64,1,160]{2,0,1:T(8,128)(2,1)S(1)}, bf16[64,1,160]{2,0,1:T(8,128)(2,1)S(1)}, u32[]{:S(2)}, u32[]{:S(2)}) %collective-permute-start.10) | collective-permute-done | bytes 20512 | tf_op jit(solution)/shard_map/ppermute | solution.py:26
  70.7 0.5 fusion.28
  71.2 1.9 collective-permute-start.11
  73.1 0.6 fusion.108
  73.7 3.9 %collective-permute-start.12 = (bf16[64,1,160]{2,0,1:T(8,128)(2,1)S(1)}, bf16[64,1,160]{2,0,1:T(8,128)(2,1)S(1)}, u32[]{:S(2)}, u32[]{:S(2)}) collective-permute-start(bf16[64,1,160]{2,0,1:T(8,128)(2,1)S(1)} %get-tuple-element.5), channel_id=1, source_target_pairs={{0,16},{16,32},{32,48},{48,64},{64,80},{80,96},{96,112},{112,128},... | collective-permute-start | bytes 61448 | tf_op jit(solution)/shard_map/ppermute | solution.py:26
  77.6 0.5 convolution_add_fusion.1
  78.2 3.4 %collective-permute-done.12 = bf16[64,1,160]{2,0,1:T(8,128)(2,1)S(1)} collective-permute-done((bf16[64,1,160]{2,0,1:T(8,128)(2,1)S(1)}, bf16[64,1,160]{2,0,1:T(8,128)(2,1)S(1)}, u32[]{:S(2)}, u32[]{:S(2)}) %collective-permute-start.12) | collective-permute-done | bytes 20512 | tf_op jit(solution)/shard_map/ppermute | solution.py:26
  81.6 0.5 fusion.29
  82.1 0.3 copy.11
  82.4 0.7 reshape.66
  83.2 0.5 stack.3
  83.7 67.4 %all_to_all.20 = bf16[16,64,2560]{2,1,0:T(8,128)(2,1)S(1)} all-to-all(bf16[16,64,2560]{2,1,0:T(8,128)(2,1)S(1)} %stack.3), channel_id=1, replica_groups=mesh['elem'=32,'band'=16] {'band'}, dimensions={0} | all-to-all | bytes 10485760 | tf_op jit(solution)/shard_map/all_to_all | solution.py:129
  151.1 1.7 convolution_bitcast_fusion
  152.8 0.1 copy.14
  152.8 0.6 copy-done.1
  153.4 1.1 multiply_reduce_fusion
  154.5 0.1 reduce_sum.21
  154.6 0.4 all_to_all.14
  155.0 26.7 %all_to_all.21 = f32[32,1,2080]{2,1,0:T(1,128)S(1)} all-to-all(f32[32,1,2080]{2,1,0:T(1,128)S(1)} %all_to_all.14), channel_id=1, replica_groups=mesh['elem'=32,'band'=16] {'elem'}, dimensions={0} | all-to-all | bytes 532480 | tf_op jit(solution)/shard_map/all_to_all | solution.py:39
  181.7 0.2 reduce_sum.22
  181.8 0.9 broadcast_in_dim.5
  182.7 3.9 %all-to-all-start.2 = ((f32[32,1,2080]{2,1,0:T(1,128)}), f32[32,1,2080]{2,1,0:T(1,128)S(1)}, u32[]{:S(2)}, u32[]{:S(2)}) async-start(f32[32,1,2080]{2,1,0:T(1,128)} %broadcast_in_dim.5), calls=%async_computation.2 | async-start | bytes 557056 | tf_op jit(solution)/shard_map/all_to_all | solution.py:56
  186.6 22.2 %all-to-all-done.2 = f32[32,1,2080]{2,1,0:T(1,128)S(1)} async-done(((f32[32,1,2080]{2,1,0:T(1,128)}), f32[32,1,2080]{2,1,0:T(1,128)S(1)}, u32[]{:S(2)}, u32[]{:S(2)}) %all-to-all-start.2) | async-done | bytes 266272 | tf_op jit(solution)/shard_map/all_to_all | solution.py:56
  208.8 0.7 reduce.2
  209.4 0.3 slice.126
  209.7 0.2 reshape.69
  209.9 0.1 dynamic_slice.3
  210.0 4.3 %convolution_convert_fusion = bf16[64,2560]{1,0:T(8,128)(2,1)} fusion(bf16[1024,2560]{1,0:T(8,128)(2,1)} %bitcast.87, f32[65,1024]{1,0:T(8,128)S(1)} %slice.126, f32[1024]{0:T(1024)S(1)} %get-tuple-element.18, f32[64]{0:T(128)S(1)} %dynamic_slice.3, s32[64]{0:T(128)S(1)} %iota_add_fusion, f32[1024]{0:T(1024)S(1)} %get-tuple-element.17), kind=kOutput, calls=%fused_computation.1 | convolution fusion | flops 336232448 | bytes 5841920 | tf_op jit(solution)/shard_map/dot_general | solution.py:139
  (23 shorter events, 0.1 us)
Async XLA Ops:
  0.0 19.1 %copy-start = (bf16[16,160,160]{2,1,0:T(8,128)(2,1)S(1)}, bf16[16,160,160]{2,1,0:T(8,128)(2,1)}, u32[]{:S(2)}) copy-start(bf16[16,160,160]{2,1,0:T(8,128)(2,1)} %param.7) | copy-start | bytes 2457604
  0.0 15.0 %copy-start.3 = (s32[16]{0:T(128)S(1)}, s32[16]{0:T(128)}, u32[]{:S(2)}) copy-start(s32[16]{0:T(128)} %param.6) | copy-start | bytes 196
  0.0 15.0 %copy-start.2 = (bf16[16,160,160]{2,1,0:T(8,128)(2,1)S(1)}, bf16[16,160,160]{2,1,0:T(8,128)(2,1)}, u32[]{:S(2)}) copy-start(bf16[16,160,160]{2,1,0:T(8,128)(2,1)} %param.8) | copy-start | bytes 2457604
  2.7 17.1 %collective-permute-start = (bf16[64,1,160]{2,0,1:T(8,128)(2,1)S(1)}, bf16[64,1,160]{2,0,1:T(8,128)(2,1)S(1)}, u32[]{:S(2)}, u32[]{:S(2)}) collective-permute-start(bf16[64,1,160]{2,0,1:T(8,128)(2,1)S(1)} %get-tuple-element.16), channel_id=1, source_target_pairs={{16,0},{32,16},{48,32},{64,48},{80,64},{96,80},{112,96},{128,112},... | collective-permute-start | bytes 61448 | tf_op jit(solution)/shard_map/ppermute | solution.py:27
  15.2 9.8 %collective-permute-start.2 = (bf16[160,160]{1,0:T(8,128)(2,1)S(1)}, bf16[160,160]{1,0:T(8,128)(2,1)S(1)}, u32[]{:S(2)}, u32[]{:S(2)}) collective-permute-start(bf16[160,160]{1,0:T(8,128)(2,1)S(1)} %slice_bitcast_fusion), channel_id=1, source_target_pairs={{0,16},{16,32},{32,48},{48,64},{64,80},{80,96},{96,112},{112,128},... | collective-permute-start | bytes 153608 | tf_op jit(solution)/shard_map/ppermute | solution.py:16
  17.2 7.9 %collective-permute-start.1 = (bf16[64,1,160]{2,0,1:T(8,128)(2,1)S(1)}, bf16[64,1,160]{2,0,1:T(8,128)(2,1)S(1)}, u32[]{:S(2)}, u32[]{:S(2)}) collective-permute-start(bf16[64,1,160]{2,0,1:T(8,128)(2,1)S(1)} %get-tuple-element.15), channel_id=1, source_target_pairs={{0,16},{16,32},{32,48},{48,64},{64,80},{80,96},{96,112},{112,128},... | collective-permute-start | bytes 61448 | tf_op jit(solution)/shard_map/ppermute | solution.py:26
  25.5 6.4 %collective-permute-start.3 = (bf16[64,1,160]{2,0,1:T(8,128)(2,1)S(1)}, bf16[64,1,160]{2,0,1:T(8,128)(2,1)S(1)}, u32[]{:S(2)}, u32[]{:S(2)}) collective-permute-start(bf16[64,1,160]{2,0,1:T(8,128)(2,1)S(1)} %get-tuple-element.14), channel_id=1, source_target_pairs={{16,0},{32,16},{48,32},{64,48},{80,64},{96,80},{112,96},{128,112},... | collective-permute-start | bytes 61448 | tf_op jit(solution)/shard_map/ppermute | solution.py:27
  30.0 7.9 %collective-permute-start.4 = (bf16[64,1,160]{2,0,1:T(8,128)(2,1)S(1)}, bf16[64,1,160]{2,0,1:T(8,128)(2,1)S(1)}, u32[]{:S(2)}, u32[]{:S(2)}) collective-permute-start(bf16[64,1,160]{2,0,1:T(8,128)(2,1)S(1)} %get-tuple-element.13), channel_id=1, source_target_pairs={{0,16},{16,32},{32,48},{48,64},{64,80},{80,96},{96,112},{112,128},... | collective-permute-start | bytes 61448 | tf_op jit(solution)/shard_map/ppermute | solution.py:26
  38.5 6.4 %collective-permute-start.5 = (bf16[64,1,160]{2,0,1:T(8,128)(2,1)S(1)}, bf16[64,1,160]{2,0,1:T(8,128)(2,1)S(1)}, u32[]{:S(2)}, u32[]{:S(2)}) collective-permute-start(bf16[64,1,160]{2,0,1:T(8,128)(2,1)S(1)} %get-tuple-element.12), channel_id=1, source_target_pairs={{16,0},{32,16},{48,32},{64,48},{80,64},{96,80},{112,96},{128,112},... | collective-permute-start | bytes 61448 | tf_op jit(solution)/shard_map/ppermute | solution.py:27
  40.9 7.9 %collective-permute-start.6 = (bf16[64,1,160]{2,0,1:T(8,128)(2,1)S(1)}, bf16[64,1,160]{2,0,1:T(8,128)(2,1)S(1)}, u32[]{:S(2)}, u32[]{:S(2)}) collective-permute-start(bf16[64,1,160]{2,0,1:T(8,128)(2,1)S(1)} %get-tuple-element.11), channel_id=1, source_target_pairs={{0,16},{16,32},{32,48},{48,64},{64,80},{80,96},{96,112},{112,128},... | collective-permute-start | bytes 61448 | tf_op jit(solution)/shard_map/ppermute | solution.py:26
  49.4 6.4 %collective-permute-start.7 = (bf16[64,1,160]{2,0,1:T(8,128)(2,1)S(1)}, bf16[64,1,160]{2,0,1:T(8,128)(2,1)S(1)}, u32[]{:S(2)}, u32[]{:S(2)}) collective-permute-start(bf16[64,1,160]{2,0,1:T(8,128)(2,1)S(1)} %get-tuple-element.10), channel_id=1, source_target_pairs={{16,0},{32,16},{48,32},{64,48},{80,64},{96,80},{112,96},{128,112},... | collective-permute-start | bytes 61448 | tf_op jit(solution)/shard_map/ppermute | solution.py:27
  51.9 7.9 %collective-permute-start.8 = (bf16[64,1,160]{2,0,1:T(8,128)(2,1)S(1)}, bf16[64,1,160]{2,0,1:T(8,128)(2,1)S(1)}, u32[]{:S(2)}, u32[]{:S(2)}) collective-permute-start(bf16[64,1,160]{2,0,1:T(8,128)(2,1)S(1)} %get-tuple-element.9), channel_id=1, source_target_pairs={{0,16},{16,32},{32,48},{48,64},{64,80},{80,96},{96,112},{112,128},... | collective-permute-start | bytes 61448 | tf_op jit(solution)/shard_map/ppermute | solution.py:26
  60.3 6.4 %collective-permute-start.9 = (bf16[64,1,160]{2,0,1:T(8,128)(2,1)S(1)}, bf16[64,1,160]{2,0,1:T(8,128)(2,1)S(1)}, u32[]{:S(2)}, u32[]{:S(2)}) collective-permute-start(bf16[64,1,160]{2,0,1:T(8,128)(2,1)S(1)} %get-tuple-element.8), channel_id=1, source_target_pairs={{16,0},{32,16},{48,32},{64,48},{80,64},{96,80},{112,96},{128,112},... | collective-permute-start | bytes 61448 | tf_op jit(solution)/shard_map/ppermute | solution.py:27
  62.8 7.9 %collective-permute-start.10 = (bf16[64,1,160]{2,0,1:T(8,128)(2,1)S(1)}, bf16[64,1,160]{2,0,1:T(8,128)(2,1)S(1)}, u32[]{:S(2)}, u32[]{:S(2)}) collective-permute-start(bf16[64,1,160]{2,0,1:T(8,128)(2,1)S(1)} %get-tuple-element.7), channel_id=1, source_target_pairs={{0,16},{16,32},{32,48},{48,64},{64,80},{80,96},{96,112},{112,128},... | collective-permute-start | bytes 61448 | tf_op jit(solution)/shard_map/ppermute | solution.py:26
  71.2 6.4 %collective-permute-start.11 = (bf16[64,1,160]{2,0,1:T(8,128)(2,1)S(1)}, bf16[64,1,160]{2,0,1:T(8,128)(2,1)S(1)}, u32[]{:S(2)}, u32[]{:S(2)}) collective-permute-start(bf16[64,1,160]{2,0,1:T(8,128)(2,1)S(1)} %get-tuple-element.6), channel_id=1, source_target_pairs={{16,0},{32,16},{48,32},{64,48},{80,64},{96,80},{112,96},{128,112},... | collective-permute-start | bytes 61448 | tf_op jit(solution)/shard_map/ppermute | solution.py:27
  73.7 7.9 %collective-permute-start.12 = (bf16[64,1,160]{2,0,1:T(8,128)(2,1)S(1)}, bf16[64,1,160]{2,0,1:T(8,128)(2,1)S(1)}, u32[]{:S(2)}, u32[]{:S(2)}) collective-permute-start(bf16[64,1,160]{2,0,1:T(8,128)(2,1)S(1)} %get-tuple-element.5), channel_id=1, source_target_pairs={{0,16},{16,32},{32,48},{48,64},{64,80},{80,96},{96,112},{112,128},... | collective-permute-start | bytes 61448 | tf_op jit(solution)/shard_map/ppermute | solution.py:26
  151.1 2.3 %copy-start.1 = (bf16[16,64,2560]{2,1,0:T(8,128)(2,1)}, bf16[16,64,2560]{2,1,0:T(8,128)(2,1)S(1)}, u32[]{:S(2)}) copy-start(bf16[16,64,2560]{2,1,0:T(8,128)(2,1)S(1)} %all_to_all.20) | copy-start | bytes 15728644
  182.7 26.1 %all-to-all-start.2 = ((f32[32,1,2080]{2,1,0:T(1,128)}), f32[32,1,2080]{2,1,0:T(1,128)S(1)}, u32[]{:S(2)}, u32[]{:S(2)}) async-start(f32[32,1,2080]{2,1,0:T(1,128)} %broadcast_in_dim.5), calls=%async_computation.2 | async-start | bytes 557056 | tf_op jit(solution)/shard_map/all_to_all | solution.py:56
